TPU v7x, 32 devices: a whole 2x2x4 slice. The times are simulated.
32 devices in a mesh: groups: 2 (over y), row: 16 (over z, x, core).
Axes of the slice: x: 2, y: 2, z: 4, core: 2. Of those that a mesh axis runs over, the one named last changes fastest.
Arguments:
- pair_cols: bfloat16 [128, 256, 128], P(None, ('groups', 'row')), parts along dimension 1, may hold values from -410 to 410
- single: bfloat16 [256, 384], P(('groups', 'row')), parts along dimension 0, may hold values from -6 to 6
- rotation: float32 [9, 256], P(None, ('groups', 'row')), parts along dimension 1, may hold values from -1 to 1, as said below
- translation: float32 [3, 256], P(None, ('groups', 'row')), parts along dimension 1, may hold values from -6 to 6
- residue_mask: int32 [256], P('groups'), parts along dimension 0, may hold values from 0 to 1, as said below
- chain_index: int32 [256], P('groups'), parts along dimension 0, may hold values from 0 to 3, never falling along the last dimension, each value on 1 to 64 neighbouring positions
- query_weight: bfloat16 [384, 192], replicated, may hold values from -0.3125 to 0.3125
- key_weight: bfloat16 [384, 192], replicated, may hold values from -0.3125 to 0.3125
- value_weight: bfloat16 [384, 192], replicated, may hold values from -0.3125 to 0.3125
- qpoint_weight: bfloat16 [384, 144], replicated, may hold values from -0.3125 to 0.3125
- kpoint_weight: bfloat16 [384, 144], replicated, may hold values from -0.3125 to 0.3125
- vpoint_weight: bfloat16 [384, 288], replicated, may hold values from -0.3125 to 0.3125
- pair_weight: bfloat16 [12, 128], replicated, may hold values from -0.5 to 0.5
- head_weight: float32 [12], replicated, may hold values from -3 to 3
- chain_weight: float32 [12], replicated, may hold values from -6 to 6
- output_weight: bfloat16 [2112, 384], replicated, may hold values from -0.125 to 0.125
- gain_first: float32 [384], replicated, may hold values from 0.5 to 1.5
- mlp_first: bfloat16 [384, 384], replicated, may hold values from -0.3125 to 0.3125
- mlp_second: bfloat16 [384, 384], replicated, may hold values from -0.3125 to 0.3125
- mlp_third: bfloat16 [384, 384], replicated, may hold values from -0.3125 to 0.3125
- gain_second: float32 [384], replicated, may hold values from 0.5 to 1.5
- frame_weight: bfloat16 [384, 6], replicated, may hold values from -0.3125 to 0.3125
Outputs:
- single_out: float32 [256, 384], P(('groups', 'row')), parts along dimension 0
- rotation_out: float32 [9, 256], P(None, ('groups', 'row')), parts along dimension 1
- translation_out: float32 [3, 256], P(None, ('groups', 'row')), parts along dimension 1
There are 2 independent parts, one for each index of `groups`. A program takes and returns all parts, laid end to end along the dimension named above; an argument that names none is the same for every part. Nothing has to cross between parts.
Inputs may be any that keep to these rules, and one draw needn't show every extreme that they name: `residue_mask`: 1 on a leading run of at least three quarters of 128 positions, 0 after it. Each column is a rotation matrix, row-major.
All inputs are finite; a program needn't handle non-finite values.
Results may differ from a plain program's by a relative error of at most 0.02.
Values may be sent and summed in bfloat16 or wider, within the bound.
A program may use at most 64 MiB of HBM per device.

v0:
```python
import jax
import jax.numpy as jnp
from jax import lax
from jax.sharding import PartitionSpec as P

LAYERS = 2


EXACT_PRODUCT = lax.Precision.HIGHEST
LOGIT_WEIGHT = (1.0 / 3.0) ** 0.5


def to_global(points, rotation, translation):
    components = []
    for component in range(3):
        components.append(
            rotation[3 * component][:, None] * points[:, 0]
            + rotation[3 * component + 1][:, None] * points[:, 1]
            + rotation[3 * component + 2][:, None] * points[:, 2]
            + translation[component][:, None]
        )
    return jnp.stack(components, axis=1)


def to_local(points, rotation, translation):
    shifted = points - jnp.transpose(translation)[:, :, None]
    components = []
    for component in range(3):
        components.append(
            rotation[component][:, None] * shifted[:, 0]
            + rotation[3 + component][:, None] * shifted[:, 1]
            + rotation[6 + component][:, None] * shifted[:, 2]
        )
    return jnp.stack(components, axis=1)


def layer_norm(values, gain_vector):
    centered = values - jnp.mean(values, axis=-1, keepdims=True)
    variance = jnp.mean(centered * centered, axis=-1, keepdims=True)
    return centered * lax.rsqrt(variance + 1e-05) * gain_vector


def project_bias(pair_rows, pair_weight):
    return jnp.einsum("ijc,hc->ihj", pair_rows, pair_weight, preferred_element_type=jnp.float32)


def key_side(
    state_bf, rotation, translation, key_weight, value_weight, kpoint_weight, vpoint_weight
):
    key_count = state_bf.shape[0]
    keys_bf = jnp.dot(state_bf, key_weight, preferred_element_type=jnp.float32).astype(jnp.bfloat16)
    values_bf = jnp.dot(state_bf, value_weight, preferred_element_type=jnp.float32).astype(
        jnp.bfloat16
    )
    key_pts = jnp.dot(state_bf, kpoint_weight, preferred_element_type=jnp.float32).reshape(
        key_count, 3, -1
    )
    value_pts = jnp.dot(state_bf, vpoint_weight, preferred_element_type=jnp.float32).reshape(
        key_count, 3, -1
    )
    return (
        keys_bf,
        values_bf,
        to_global(key_pts, rotation, translation),
        to_global(value_pts, rotation, translation),
    )


def attend(
    state_bf,
    rotation,
    translation,
    pair_rows,
    pair_bias,
    chain_rows,
    keys_bf,
    values_bf,
    key_global,
    value_global,
    chain_index,
    residue_mask,
    query_weight,
    qpoint_weight,
    head_weight,
    chain_weight,
):
    row_count = state_bf.shape[0]
    heads = head_weight.shape[0]
    key_count = keys_bf.shape[0]
    queries = (
        jnp.dot(state_bf, query_weight, preferred_element_type=jnp.float32)
        .astype(jnp.bfloat16)
        .reshape(row_count, heads, -1)
    )
    head_dim = queries.shape[2]
    query_pts = to_global(
        jnp.dot(state_bf, qpoint_weight, preferred_element_type=jnp.float32).reshape(
            row_count, 3, -1
        ),
        rotation,
        translation,
    )
    query_pts = query_pts.reshape(row_count, 3, heads, -1)
    key_pts = key_global.reshape(key_count, 3, heads, -1)
    point_count = query_pts.shape[3]
    scores = jnp.einsum(
        "ihd,jhd->ihj",
        queries,
        keys_bf.reshape(key_count, heads, head_dim),
        preferred_element_type=jnp.float32,
    )
    cross_term = jnp.einsum("ikhp,jkhp->ihj", query_pts, key_pts, precision=EXACT_PRODUCT)
    query_square = jnp.sum(query_pts * query_pts, axis=(1, 3))
    key_square = jnp.sum(key_pts * key_pts, axis=(1, 3))
    distance = query_square[:, :, None] + jnp.transpose(key_square)[None] - 2.0 * cross_term
    weight_c = (2.0 / (9.0 * point_count)) ** 0.5
    point_scale = jax.nn.softplus(head_weight)
    same_chain = (chain_rows[:, None] == chain_index[None, :]).astype(jnp.float32)
    logits = LOGIT_WEIGHT * (
        scores * head_dim ** (-0.5)
        + pair_bias
        - (0.5 * weight_c * point_scale)[None, :, None] * distance
    )
    logits = (
        logits
        + chain_weight[None, :, None] * same_chain[:, None, :]
        + ((residue_mask.astype(jnp.float32) - 1.0) * 100000.0)[None, None, :]
    )
    attention = jax.nn.softmax(logits, axis=-1).astype(jnp.bfloat16)
    outputs = jnp.einsum(
        "ihj,jhd->ihd",
        attention,
        values_bf.reshape(key_count, heads, head_dim),
        preferred_element_type=jnp.float32,
    )
    value_pts = value_global.reshape(key_count, 3, heads, -1)
    point_glob = jnp.einsum(
        "ihj,jkhp->ikhp", attention.astype(jnp.float32), value_pts, precision=EXACT_PRODUCT
    )
    point_local = to_local(point_glob.reshape(row_count, 3, -1), rotation, translation)
    point_norms = jnp.sqrt(jnp.sum(point_local * point_local, axis=1) + 1e-08)
    pair_out = jnp.einsum("ihj,ijc->ihc", attention, pair_rows, preferred_element_type=jnp.float32)
    return jnp.concatenate(
        [
            outputs.reshape(row_count, -1),
            point_local.reshape(row_count, -1),
            point_norms,
            pair_out.reshape(row_count, -1),
        ],
        axis=1,
    ).astype(jnp.bfloat16)


def frame_compose(rotation, translation, frame_update):
    inverse = lax.rsqrt(1.0 + jnp.sum(frame_update[:, :3] * frame_update[:, :3], axis=1))
    vector_x = frame_update[:, 0] * inverse
    vector_y = frame_update[:, 1] * inverse
    vector_z = frame_update[:, 2] * inverse
    turn_matrix = [
        [
            inverse * inverse + vector_x * vector_x - vector_y * vector_y - vector_z * vector_z,
            2.0 * (vector_x * vector_y - inverse * vector_z),
            2.0 * (vector_x * vector_z + inverse * vector_y),
        ],
        [
            2.0 * (vector_x * vector_y + inverse * vector_z),
            inverse * inverse - vector_x * vector_x + vector_y * vector_y - vector_z * vector_z,
            2.0 * (vector_y * vector_z - inverse * vector_x),
        ],
        [
            2.0 * (vector_x * vector_z - inverse * vector_y),
            2.0 * (vector_y * vector_z + inverse * vector_x),
            inverse * inverse - vector_x * vector_x - vector_y * vector_y + vector_z * vector_z,
        ],
    ]
    new_rotation = jnp.stack(
        [
            rotation[3 * outer] * turn_matrix[0][inner]
            + rotation[3 * outer + 1] * turn_matrix[1][inner]
            + rotation[3 * outer + 2] * turn_matrix[2][inner]
            for outer in range(3)
            for inner in range(3)
        ]
    )
    new_translation = jnp.stack(
        [
            rotation[3 * outer] * frame_update[:, 3]
            + rotation[3 * outer + 1] * frame_update[:, 4]
            + rotation[3 * outer + 2] * frame_update[:, 5]
            + translation[outer]
            for outer in range(3)
        ]
    )
    return (new_rotation, new_translation)


def update(
    single_state,
    concat,
    rotation,
    translation,
    output_weight,
    gain_first,
    mlp_first,
    mlp_second,
    mlp_third,
    gain_second,
    frame_weight,
):
    single_state = single_state + jnp.dot(concat, output_weight, preferred_element_type=jnp.float32)
    normed = layer_norm(single_state, gain_first)
    hidden = jax.nn.relu(
        jnp.dot(normed.astype(jnp.bfloat16), mlp_first, preferred_element_type=jnp.float32)
    ).astype(jnp.bfloat16)
    hidden = jax.nn.relu(jnp.dot(hidden, mlp_second, preferred_element_type=jnp.float32)).astype(
        jnp.bfloat16
    )
    single_state = layer_norm(
        normed + jnp.dot(hidden, mlp_third, preferred_element_type=jnp.float32), gain_second
    )
    state_bf = single_state.astype(jnp.bfloat16)
    frame_update = jnp.dot(state_bf, frame_weight, preferred_element_type=jnp.float32)
    new_rotation, new_translation = frame_compose(rotation, translation, frame_update)
    return (single_state, state_bf, new_rotation, new_translation)


def on_device(
    pair_cols,
    single,
    rotation,
    translation,
    residue_mask,
    chain_index,
    query_weight,
    key_weight,
    value_weight,
    qpoint_weight,
    kpoint_weight,
    vpoint_weight,
    pair_weight,
    head_weight,
    chain_weight,
    output_weight,
    gain_first,
    mlp_first,
    mlp_second,
    mlp_third,
    gain_second,
    frame_weight,
):
    axis_size = lax.axis_size("row")
    row_count = single.shape[0]
    row_start = lax.axis_index("row") * row_count
    blocks = pair_cols.reshape(axis_size, row_count, pair_cols.shape[1], pair_cols.shape[2])
    arrived = lax.all_to_all(blocks, "row", split_axis=0, concat_axis=2, tiled=True)[0]
    pair_bias = project_bias(arrived, pair_weight)
    chain_rows = lax.dynamic_slice_in_dim(chain_index, row_start, row_count)
    single_state = single.astype(jnp.float32)
    state_bf = single
    channels = single.shape[1]
    for layer_index in range(LAYERS):
        packed = jnp.concatenate(
            [state_bf.astype(jnp.float32), jnp.transpose(rotation), jnp.transpose(translation)],
            axis=1,
        )
        gathered = lax.all_gather(packed, "row", axis=0, tiled=True)
        single_all = gathered[:, :channels].astype(jnp.bfloat16)
        rotation_all = jnp.transpose(gathered[:, channels : channels + 9])
        translation_all = jnp.transpose(gathered[:, channels + 9 : channels + 12])
        keys_bf, values_bf, key_global, value_global = key_side(
            single_all,
            rotation_all,
            translation_all,
            key_weight,
            value_weight,
            kpoint_weight,
            vpoint_weight,
        )
        concat = attend(
            state_bf,
            rotation,
            translation,
            arrived,
            pair_bias,
            chain_rows,
            keys_bf,
            values_bf,
            key_global,
            value_global,
            chain_index,
            residue_mask,
            query_weight,
            qpoint_weight,
            head_weight,
            chain_weight,
        )
        single_state, state_bf, rotation, translation = update(
            single_state,
            concat,
            rotation,
            translation,
            output_weight,
            gain_first,
            mlp_first,
            mlp_second,
            mlp_third,
            gain_second,
            frame_weight,
        )
    return (single_state, rotation, translation)


def solution(mesh):
    return jax.shard_map(
        on_device,
        mesh=mesh,
        in_specs=(
            P(None, ("groups", "row"), None),
            P(("groups", "row"), None),
            P(None, ("groups", "row")),
            P(None, ("groups", "row")),
            P("groups"),
            P("groups"),
            P(),
            P(),
            P(),
            P(),
            P(),
            P(),
            P(),
            P(),
            P(),
            P(),
            P(),
            P(),
            P(),
            P(),
            P(),
            P(),
        ),
        out_specs=(
            P(("groups", "row"), None),
            P(None, ("groups", "row")),
            P(None, ("groups", "row")),
        ),
        check_vma=False,
    )
```

profile of v0, /device:TPU:0, one launch (start us, length us, event | category | flops | bytes accessed | tf_op | source)
XLA Modules:
  0.0 73.3 jit_solution(4515566459287455131)
XLA Ops:
  0.7 7.5 %all-to-all-start = ((bf16[16,8,8,128]{3,2,1,0:T(8,128)(2,1)}), bf16[16,8,8,128]{3,2,1,0:T(8,128)(2,1)S(1)}, u32[]{:S(2)}, u32[]{:S(2)}) async-start(bf16[16,8,8,128]{3,2,1,0:T(8,128)(2,1)} %bitcast.557), calls=%async_computation | async-start | bytes 524288 | tf_op jit(solution)/shard_map/all_to_all | solution.py:255
  8.2 0.8 %copy.283 = f32[3,8]{0,1:T(8,128)S(1)} copy(f32[3,8]{1,0:T(4,128)} %param.25) | data formatting | bytes 192 | tf_op args[3]
  9.0 0.7 convert_element_type.73
  9.7 1.4 %slice_reduce_fusion.26 = (f32[8]{0:T(128)S(1)}, f32[8]{0:T(128)S(1)}, f32[8]{0:T(128)S(1)}, f32[8]{0:T(128)S(1)}, f32[8]{0:T(128)S(1)}, /*index=5*/f32[8]{0:T(1...) fusion(f32[3,8]{0,1:T(8,128)S(1)} %copy.283, ...), kind=kLoop, calls=%fused_computation.230 | loop fusion | bytes 768 | tf_op jit(solution)/shard_map/slice | solution.py:20
  11.1 0.8 %pad_maximum_fusion.8 = f32[8,396]{1,0:T(8,128)S(1)} fusion(f32[8,3]{1,0:T(8,128)S(1)} %bitcast.555, f32[8,9]{1,0:T(8,128)} %bitcast.546, f32[8,384]{1,0:T(8,128)S(1)} %convert_element_type.73), kind=kLoop, calls=%fused_computation.135 | loop fusion | flops 6336 | bytes 25344 | tf_op jit(solution)/shard_map/concatenate | solution.py:262
  11.9 22.5 %all_gather.6 = f32[128,396]{1,0:T(8,128)S(1)} all-gather(f32[8,396]{1,0:T(8,128)S(1)} %pad_maximum_fusion.8), channel_id=1, replica_groups=mesh['groups'=2,'row'=16] {'row'}, dimensions={0}, use_global_device_ids=true | all-gather | bytes 215424 | tf_op jit(solution)/shard_map/all_gather | solution.py:266
  34.5 1.1 %fusion.141 = f32[128,144]{0,1:T(8,128)S(1)} fusion(bf16[384,144]{0,1:T(8,128)(2,1)} %param.32, f32[128,396]{1,0:T(8,128)S(1)} %all_gather.6), kind=kOutput, calls=%fused_computation.377 | convolution fusion | flops 14155776 | bytes 282624 | tf_op jit(solution)/shard_map/dot_general | solution.py:55
  35.9 0.5 slice_reduce_fusion.20
  37.5 0.4 fusion.21
  38.8 0.3 fusion.131
  39.2 0.3 convolution_bitcast_fusion.1
  40.6 0.4 fusion.132
  41.3 1.4 %fusion.32 = bf16[8,384]{1,0:T(8,128)(2,1)S(1)} fusion(bf16[384,384]{1,0:T(8,128)(2,1)} %param.40, bf16[384,384]{1,0:T(8,128)(2,1)} %param.39, f32[8,384]{1,0:T(8,128)S(1)} %get-tuple-element.198, f32[384]{0:T(512)S(1)} %copy-done.17, f32[8]{0:T(128)S(1)} %add_rsqrt_fusion.4, f32[8]{0:T(128)S(1)} %broadcast_multiply_fusion.3), kind=kOutput, calls=%fused_computation.54 | convolution fusion | flops 4743168 | bytes 609856 | tf_op jit(solution)/shard_map/dot_general | solution.py:215
  42.6 1.2 %fusion.133 = (f32[8]{0:T(128)S(1)}, f32[8,384]{1,0:T(8,128)S(1)}) fusion(bf16[8,384]{1,0:T(8,128)(2,1)S(1)} %fusion.32, bf16[384,384]{1,0:T(8,128)(2,1)} %param.41, f32[384]{0:T(512)S(1)} %copy-done.17, f32[8]{0:T(128)S(1)} %add_rsqrt_fusion.4, f32[8,384]{1,0:T(8,128)S(1)} %get-tuple-element.198, f32[8]{0:T(128)S(1)} %broadcast_multiply_fusion.3), kind=kOutput, calls=%fused_computation.373 | convolution fusion | flops 2374648 | bytes 327264 | tf_op jit(solution)/shard_map/dot_general | solution.py:219
  45.5 18.1 %all_gather.7 = f32[128,396]{1,0:T(8,128)S(1)} all-gather(f32[8,396]{1,0:T(8,128)S(1)} %pad_maximum_fusion.9), channel_id=1, replica_groups=mesh['groups'=2,'row'=16] {'row'}, dimensions={0}, use_global_device_ids=true | all-gather | bytes 215424 | tf_op jit(solution)/shard_map/all_gather | solution.py:266
  65.1 0.4 slice_reduce_fusion.11
  66.4 0.4 fusion.25
  66.7 0.3 fusion.134
  67.2 0.3 convolution_bitcast_fusion
  68.6 0.4 fusion.135
  69.2 0.3 fusion.33
  69.6 1.2 %fusion.136 = (f32[8]{0:T(128)S(1)}, f32[8,384]{1,0:T(8,128)S(1)}) fusion(bf16[8,384]{1,0:T(8,128)(2,1)S(1)} %fusion.33, bf16[384,384]{1,0:T(8,128)(2,1)} %param.41, f32[384]{0:T(512)S(1)} %copy-done.17, f32[8]{0:T(128)S(1)} %add_rsqrt_fusion.1, f32[8,384]{1,0:T(8,128)S(1)} %get-tuple-element.204, f32[8]{0:T(128)S(1)} %broadcast_multiply_fusion.1), kind=kOutput, calls=%fused_computation.376 | convolution fusion | flops 2374648 | bytes 327264 | tf_op jit(solution)/shard_map/dot_general | solution.py:219
  71.9 0.7 copy.359
  72.6 0.7 stack.148
  (170 shorter events, 9.8 us)
Async XLA Ops:
  0.6 40.0 %copy-start = (bf16[2112,384]{1,0:T(8,128)(2,1)S(1)}, bf16[2112,384]{1,0:T(8,128)(2,1)}, u32[]{:S(2)}) copy-start(bf16[2112,384]{1,0:T(8,128)(2,1)} %param.37) | copy-start | bytes 4866052
  0.6 34.9 %copy-start.2 = (bf16[384,288]{0,1:T(8,128)(2,1)S(1)}, bf16[384,288]{0,1:T(8,128)(2,1)}, u32[]{:S(2)}) copy-start(bf16[384,288]{0,1:T(8,128)(2,1)} %param.33) | copy-start | bytes 663556
  0.7 37.9 %all-to-all-start = ((bf16[16,8,8,128]{3,2,1,0:T(8,128)(2,1)}), bf16[16,8,8,128]{3,2,1,0:T(8,128)(2,1)S(1)}, u32[]{:S(2)}, u32[]{:S(2)}) async-start(bf16[16,8,8,128]{3,2,1,0:T(8,128)(2,1)} %bitcast.557), calls=%async_computation | async-start | bytes 524288 | tf_op jit(solution)/shard_map/all_to_all | solution.py:255
  8.2 28.3 %copy-start.7 = (bf16[384,144]{0,1:T(8,128)(2,1)S(1)}, bf16[384,144]{0,1:T(8,128)(2,1)}, u32[]{:S(2)}) copy-start(bf16[384,144]{0,1:T(8,128)(2,1)} %param.31) | copy-start | bytes 331780
  8.2 28.3 %copy-start.8 = (bf16[8,384]{1,0:T(8,128)(2,1)S(1)}, bf16[8,384]{1,0:T(8,128)(2,1)}, u32[]{:S(2)}) copy-start(bf16[8,384]{1,0:T(8,128)(2,1)} %param.23) | copy-start | bytes 18436
  11.9 25.2 %copy-start.18 = (f32[12]{0:T(128)S(1)}, f32[12]{0:T(128)}, u32[]{:S(2)}) copy-start(f32[12]{0:T(128)} %param.35) | copy-start | bytes 148
  11.9 25.3 %copy-start.5 = (bf16[384,192]{0,1:T(8,128)(2,1)S(1)}, bf16[384,192]{0,1:T(8,128)(2,1)}, u32[]{:S(2)}) copy-start(bf16[384,192]{0,1:T(8,128)(2,1)} %param.28) | copy-start | bytes 442372
  34.4 2.9 %copy-start.14 = (s32[128]{0:T(128)S(1)}, s32[128]{0:T(128)}, u32[]{:S(2)}) copy-start(s32[128]{0:T(128)} %param.27) | copy-start | bytes 1540
  35.6 2.3 %copy-start.19 = (s32[128]{0:T(128)S(1)}, s32[128]{0:T(128)}, u32[]{:S(2)}) copy-start(s32[128]{0:T(128)} %param.26) | copy-start | bytes 1540
  35.6 2.5 %copy-start.3 = (bf16[384,192]{0,1:T(8,128)(2,1)S(1)}, bf16[384,192]{0,1:T(8,128)(2,1)}, u32[]{:S(2)}) copy-start(bf16[384,192]{0,1:T(8,128)(2,1)} %param.30) | copy-start | bytes 442372
  35.9 2.5 %copy-start.4 = (bf16[384,192]{0,1:T(8,128)(2,1)S(1)}, bf16[384,192]{0,1:T(8,128)(2,1)}, u32[]{:S(2)}) copy-start(bf16[384,192]{0,1:T(8,128)(2,1)} %param.29) | copy-start | bytes 442372
  35.9 2.7 %copy-start.12 = (bf16[12,128]{1,0:T(8,128)(2,1)S(1)}, bf16[12,128]{1,0:T(8,128)(2,1)}, u32[]{:S(2)}) copy-start(bf16[12,128]{1,0:T(8,128)(2,1)} %param.34) | copy-start | bytes 9220
  36.4 2.4 %copy-start.13 = (f32[12]{0:T(128)S(1)}, f32[12]{0:T(128)}, u32[]{:S(2)}) copy-start(f32[12]{0:T(128)} %param.36) | copy-start | bytes 148
  39.2 2.1 %copy-start.17 = (f32[384]{0:T(512)S(1)}, f32[384]{0:T(512)}, u32[]{:S(2)}) copy-start(f32[384]{0:T(512)} %param.38) | copy-start | bytes 4612
  40.1 4.0 %copy-start.11 = (f32[384]{0:T(512)S(1)}, f32[384]{0:T(512)}, u32[]{:S(2)}) copy-start(f32[384]{0:T(512)} %param.42) | copy-start | bytes 4612
  40.2 4.0 %copy-start.10 = (bf16[384,6]{0,1:T(8,128)(2,1)S(1)}, bf16[384,6]{0,1:T(8,128)(2,1)}, u32[]{:S(2)}) copy-start(bf16[384,6]{0,1:T(8,128)(2,1)} %param.43) | copy-start | bytes 13828
  40.3 4.7 %copy-start.1 = (f32[9,8]{0,1:T(8,128)S(1)}, f32[9,8]{0,1:T(8,128)}, u32[]{:S(2)}) copy-start(f32[9,8]{0,1:T(8,128)} %param.24) | copy-start | bytes 868
  40.6 23.2 %copy-start.6 = (bf16[384,144]{0,1:T(8,128)(2,1)S(1)}, bf16[384,144]{0,1:T(8,128)(2,1)}, u32[]{:S(2)}) copy-start(bf16[384,144]{0,1:T(8,128)(2,1)} %param.32) | copy-start | bytes 331780
  67.1 2.1 %copy-start.15 = (bf16[384,384]{1,0:T(8,128)(2,1)S(1)}, bf16[384,384]{1,0:T(8,128)(2,1)}, u32[]{:S(2)}) copy-start(bf16[384,384]{1,0:T(8,128)(2,1)} %param.40) | copy-start | bytes 884740
  67.2 2.1 %copy-start.16 = (bf16[384,384]{1,0:T(8,128)(2,1)S(1)}, bf16[384,384]{1,0:T(8,128)(2,1)}, u32[]{:S(2)}) copy-start(bf16[384,384]{1,0:T(8,128)(2,1)} %param.39) | copy-start | bytes 884740
  71.1 2.2 %copy-start.9 = (f32[8,384]{1,0:T(8,128)}, f32[8,384]{1,0:T(8,128)S(1)}, u32[]{:S(2)}) copy-start(f32[8,384]{1,0:T(8,128)S(1)} %multiply_multiply_fusion) | copy-start | bytes 36868
where the time goes:
time: 73.8 us; the launch traced here: 73.3 us
  blocking collectives  40.7 us (55%)
  matrix products  11.1 us (15%)
  local copies, waits for them, and re-layouts  8.4 us (11%)
  starting transfers between devices  7.53 us (10%)
  other arithmetic  4.2 us (6%)
  between operations  1.37 us (2%)
    all_gather x2, blocking collectives, on_device(): gathered = lax.all_gather(packed, 'row', axis=0, tiled=True)  40.7 us
    all_to_all x1, starting transfers between devices, on_device(): lax.all_to_all(blocks, 'row', split_axis=0, concat_axis=2, tiled=True)[0]  7.53 us
    dot_general x2, matrix products, update(): jnp.dot(hidden, mlp_third, preferred_element_type=jnp.float32)  2.49 us
    slice x3, local copies, waits for them, and re-layouts, to_global(): translation[component][:, None]  2.07 us
    dot_general x2, matrix products, update(): jnp.dot(hidden, mlp_second, preferred_element_type=jnp.float32)  1.7 us
    unnamed x44, local copies, waits for them, and re-layouts  1.62 us
  transfers between devices with their start and end apart: 1, of which 0 were waited for; matrix products, arithmetic and copies ran while one was open for 10% of the time, Pallas kernels for 0%

commit v1 on v0

v1 whole, which is shorter than its diff:
```python
import functools

import jax
import jax.numpy as jnp
from jax import lax
from jax.experimental import pallas as pl
from jax.experimental.pallas import tpu as pltpu
from jax.sharding import PartitionSpec as P

(
    PAIR_COLS,
    SINGLE,
    ROTATION,
    TRANSLATION,
    RESIDUE_MASK,
    CHAIN_INDEX,
    QUERY_WEIGHT,
    KEY_WEIGHT,
    VALUE_WEIGHT,
    QPOINT_WEIGHT,
    KPOINT_WEIGHT,
    VPOINT_WEIGHT,
    PAIR_WEIGHT,
    HEAD_WEIGHT,
    CHAIN_WEIGHT,
    OUTPUT_WEIGHT,
    GAIN_FIRST,
    MLP_FIRST,
    MLP_SECOND,
    MLP_THIRD,
    GAIN_SECOND,
    FRAME_WEIGHT,
) = range(22)
LAYERS = 2
LOGIT_WEIGHT = (1.0 / 3.0) ** 0.5
LANES = 128
HALF = 64
BF = jnp.bfloat16
F32 = jnp.float32
MESH = pl.DeviceIdType.MESH


def up(value, multiple):
    return -(-value // multiple) * multiple


def iota(shape, dim):
    return lax.broadcasted_iota(jnp.int32, shape, dim)


def dot(left, right):
    return jnp.dot(left, right, preferred_element_type=F32)


def dot_t(left, right):
    return lax.dot_general(left, right, (((1,), (1,)), ((), ())), preferred_element_type=F32)


def high_low(values):
    high = values.astype(BF).astype(F32)
    return high, values - high


def layer_norm(values, gain):
    centered = values - jnp.mean(values, axis=-1, keepdims=True)
    variance = jnp.mean(centered * centered, axis=-1, keepdims=True)
    return centered * lax.rsqrt(variance + 1e-05) * gain


def columns_of(frame):
    return [frame[:, c : c + 1] for c in range(12)]


def rotate(frame, parts):
    return [
        frame[3 * c] * parts[0]
        + frame[3 * c + 1] * parts[1]
        + frame[3 * c + 2] * parts[2]
        + frame[9 + c]
        for c in range(3)
    ]


def compose(frame, upd):
    inverse = lax.rsqrt(1.0 + (upd[0] * upd[0] + upd[1] * upd[1] + upd[2] * upd[2]))
    w, x, y, z = inverse, upd[0] * inverse, upd[1] * inverse, upd[2] * inverse
    turn = [
        [w * w + x * x - y * y - z * z, 2.0 * (x * y - w * z), 2.0 * (x * z + w * y)],
        [2.0 * (x * y + w * z), w * w - x * x + y * y - z * z, 2.0 * (y * z - w * x)],
        [2.0 * (x * z - w * y), 2.0 * (y * z + w * x), w * w - x * x - y * y + z * z],
    ]
    rotation = [
        frame[3 * a] * turn[0][b] + frame[3 * a + 1] * turn[1][b] + frame[3 * a + 2] * turn[2][b]
        for a in range(3)
        for b in range(3)
    ]
    translation = [
        frame[3 * a] * upd[3] + frame[3 * a + 1] * upd[4] + frame[3 * a + 2] * upd[5] + frame[9 + a]
        for a in range(3)
    ]
    return rotation + translation


def pack_frame(frame):
    high, rest = high_low(frame)
    middle, low = high_low(rest)
    return (high + pltpu.roll(middle, 16, 1) + pltpu.roll(low, 32, 1)).astype(BF)


def unpack_frame(packed):
    return packed + pltpu.roll(packed, LANES - 16, 1) + pltpu.roll(packed, LANES - 32, 1)


def kernel(n, names, *refs):
    count = len(names)
    hbm = dict(zip(names, refs[:count]))
    single_out, rotation_out, translation_out = refs[count : count + 3]
    rest = refs[count + 3 :]
    vm = dict(zip(names[1:], rest[: count - 1]))
    (arrived, pair_buf, gat, wkv, wq, pair_w, tile, stat, pair_acc) = rest[count - 1 : -6]
    load_sem, gsend, grecv, psend, precv, own_sem = rest[-6:]

    rows, channels = vm[SINGLE].shape
    heads = vm[HEAD_WEIGHT].shape[1]
    hp = pair_w.shape[0]
    keys = n * rows
    head_dim = hbm[QUERY_WEIGHT].shape[0] // heads
    qd = up(heads * head_dim, LANES)
    pw = hbm[KPOINT_WEIGHT].shape[0] // 3
    pv = hbm[VPOINT_WEIGHT].shape[0] // 3
    points, vpoints = pw // heads, pv // heads
    me = lax.axis_index("row")

    def each_peer(body):
        if n <= 16:
            for k in range(1, n):
                body(lax.rem(me + k, n))
        else:

            def step(k, carry):
                body(lax.rem(me + k, n))
                return carry

            lax.fori_loop(1, n, step, 0)

    base_v = qd + 3 * LANES
    placed = {
        QUERY_WEIGHT: (wq, 0, heads * head_dim, 1),
        KEY_WEIGHT: (wkv, 0, heads * head_dim, 1),
        VALUE_WEIGHT: (wkv, base_v, heads * head_dim, 1),
        QPOINT_WEIGHT: (wq, qd, pw, 3),
        KPOINT_WEIGHT: (wkv, qd, pw, 3),
        VPOINT_WEIGHT: (wkv, base_v + qd, pv, 3),
    }
    loads = {}
    used = 0
    for name in names[1:]:
        if name in placed:
            target, first, size, pieces = placed[name]
            pairs = [
                (hbm[name].at[pl.ds(c * size, size)], target.at[pl.ds(first + c * LANES, size)])
                for c in range(pieces)
            ]
        else:
            pairs = [(hbm[name], vm[name])]
        loads[name] = []
        for source, target in pairs:
            loads[name].append(pltpu.make_async_copy(source, target, load_sem.at[used]))
            used += 1

    def ready(*wanted):
        for name in wanted:
            for load in loads[name]:
                load.wait()

    for name in names[1:]:
        for load in loads[name]:
            load.start()

    barrier = pltpu.get_barrier_semaphore()
    each_peer(
        lambda p: pl.semaphore_signal(barrier, inc=1, device_id={"row": p}, device_id_type=MESH)
    )

    def send_state(layer, p):
        return pltpu.make_async_remote_copy(
            src_ref=gat.at[layer, me],
            dst_ref=gat.at[layer, me],
            send_sem=gsend.at[layer, p],
            recv_sem=grecv.at[layer, me],
            device_id={"row": p},
            device_id_type=MESH,
        )

    def take_state(layer, p):
        return pltpu.make_async_remote_copy(
            src_ref=gat.at[layer, p],
            dst_ref=gat.at[layer, p],
            send_sem=gsend.at[layer, p],
            recv_sem=grecv.at[layer, p],
            device_id={"row": p},
            device_id_type=MESH,
        )

    def send_pair(p, slot):
        return pltpu.make_async_remote_copy(
            src_ref=hbm[PAIR_COLS].at[pl.ds(p * rows, rows)],
            dst_ref=arrived.at[slot],
            send_sem=psend.at[p],
            recv_sem=precv.at[slot],
            device_id={"row": p},
            device_id_type=MESH,
        )

    own_pair = pltpu.make_async_copy(
        hbm[PAIR_COLS].at[pl.ds(me * rows, rows)], arrived.at[me], own_sem
    )
    own_pair.start()

    tile[...] = jnp.zeros_like(tile)
    ready(SINGLE, ROTATION, TRANSLATION, HEAD_WEIGHT, CHAIN_WEIGHT)
    tile[0:rows, 0:9] = vm[ROTATION][...]
    lane_rows = iota((rows, LANES), 1)
    frame = jnp.where(lane_rows < 9, tile[0:rows, :], 0.0)
    tile[9:12, 0:rows] = vm[TRANSLATION][...]
    tile[12:13, 0:heads] = vm[HEAD_WEIGHT][...]
    tile[13:14, 0:heads] = vm[CHAIN_WEIGHT][...]
    turned = tile[...].T
    frame = jnp.where((lane_rows >= 9) & (lane_rows < 12), turned[0:rows], frame)
    head_col = turned[0:hp, 12:13]
    chain_col = turned[0:hp, 13:14]
    state = vm[SINGLE][...].astype(F32)
    gat[0, me, :, 0:channels] = vm[SINGLE][...]
    gat[0, me, :, channels:] = pack_frame(frame)

    pl.semaphore_wait(barrier, n - 1)
    each_peer(lambda p: send_state(0, p).start())
    each_peer(lambda p: send_pair(p, me).start())

    for target, first, size, pieces in placed.values():
        for c in range(pieces):
            start = first + c * LANES + size
            gap = up(size, LANES) - size
            if gap:
                target[start : start + gap] = jnp.zeros((gap, channels), BF)
    pair_w[...] = jnp.zeros_like(pair_w)
    ready(PAIR_WEIGHT)
    pair_w[0:heads, :] = vm[PAIR_WEIGHT][...].astype(F32)

    mask_q = (
        (iota((hp, qd), 1) // head_dim == iota((hp, qd), 0)) & (iota((hp, qd), 1) < heads * head_dim)
    ).astype(F32)
    lane_p = iota((hp, LANES), 1) % HALF
    mask_p = ((lane_p // points == iota((hp, LANES), 0)) & (lane_p < pw)).astype(F32)
    mask_once = jnp.where(iota((hp, LANES), 1) < HALF, mask_p, 0.0)
    lane_v = iota((hp, LANES), 1)
    mask_v = ((lane_v // vpoints == iota((hp, LANES), 0)) & (lane_v < pv)).astype(F32)

    def expand(values, mask):
        return (values[:, None, :] * mask[None]).reshape(rows * hp, values.shape[1])

    def collapse(values, mask):
        return jnp.sum(values.reshape(rows, hp, values.shape[1]) * mask[None], axis=1)

    def per_row(column):
        return jnp.broadcast_to(column[None], (rows, hp, 1)).reshape(rows * hp, 1)

    softplus = jnp.maximum(head_col, 0.0) + jnp.log(1.0 + jnp.exp(-jnp.abs(head_col)))
    weight_c = (2.0 / (9.0 * points)) ** 0.5
    coef = per_row(-LOGIT_WEIGHT * 0.5 * weight_c * softplus)
    mask_rows = jnp.broadcast_to(mask_p[None], (rows, hp, LANES)).reshape(rows * hp, LANES).astype(BF)

    ready(CHAIN_INDEX, RESIDUE_MASK)
    chain = vm[CHAIN_INDEX][...].astype(F32)
    at_me = iota((rows, keys), 1) == me * rows + iota((rows, keys), 0)
    chain_own = jnp.sum(jnp.where(at_me, chain, 0.0), axis=1, keepdims=True)
    same = (chain == chain_own).astype(F32)
    masked = (vm[RESIDUE_MASK][...].astype(F32) - 1.0) * 100000.0

    state_bf = vm[SINGLE][...]
    for layer in range(LAYERS):
        cols = columns_of(frame)
        if layer == 0:
            ready(QUERY_WEIGHT, QPOINT_WEIGHT)
        own = dot_t(state_bf, wq[...])
        q_rows = expand(own[:, 0:qd].astype(BF).astype(F32), mask_q).astype(BF)
        lane_own = lane_rows < pw
        q_pts = rotate(cols, [own[:, qd + c * LANES : qd + (c + 1) * LANES] for c in range(3)])
        q_pts = [jnp.where(lane_own, part, 0.0) for part in q_pts]
        square = q_pts[0] * q_pts[0] + q_pts[1] * q_pts[1] + q_pts[2] * q_pts[2]
        q_square = jnp.sum(expand(square, mask_once), axis=1, keepdims=True)
        left_high, left_low = [], []
        for part in q_pts:
            high, low = high_low(-2.0 * part)
            left_high.append(expand(high + pltpu.roll(high, HALF, 1), mask_p).astype(BF))
            left_low.append(expand(low + pltpu.roll(low, HALF, 1), mask_p).astype(BF))
        left_high = jnp.concatenate(left_high + [mask_rows], axis=1)
        left_low = jnp.concatenate(left_low, axis=1)

        each_peer(lambda p: take_state(layer, p).wait_recv())
        every = gat[layer].astype(F32).reshape(keys, channels + LANES)
        if layer == 0:
            ready(KEY_WEIGHT, KPOINT_WEIGHT, VALUE_WEIGHT, VPOINT_WEIGHT)
        kv = dot_t(every[:, 0:channels].astype(BF), wkv[...])
        key_cols = columns_of(unpack_frame(every[:, channels:]))
        k_bf = kv[:, 0:qd].astype(BF)
        v_bf = kv[:, base_v : base_v + qd].astype(BF)
        k_pts = rotate(key_cols, [kv[:, qd + c * LANES : qd + (c + 1) * LANES] for c in range(3)])
        lane_key = iota((keys, LANES), 1) < pw
        k_pts = [jnp.where(lane_key, part, 0.0) for part in k_pts]
        k_square = k_pts[0] * k_pts[0] + k_pts[1] * k_pts[1] + k_pts[2] * k_pts[2]
        right = []
        for part in k_pts + [k_square]:
            high, low = high_low(part)
            right.append((high + pltpu.roll(low, HALF, 1)).astype(BF))
        start = base_v + qd
        v_pts = rotate(
            key_cols, [kv[:, start + c * LANES : start + (c + 1) * LANES] for c in range(3)]
        )
        v_high = jnp.concatenate([part.astype(BF) for part in v_pts], axis=1)
        v_low = jnp.concatenate([high_low(part)[1].astype(BF) for part in v_pts], axis=1)
        distance = (
            q_square
            + dot_t(left_high, jnp.concatenate(right, axis=1))
            + dot_t(left_low, jnp.concatenate(right[0:3], axis=1))
        )
        scores = dot_t(q_rows, k_bf)

        if layer == 0:
            own_pair.wait()
            each_peer(lambda p: send_pair(p, p).wait_recv())
            w16 = pair_w[...].astype(BF)
            for i in range(rows):
                block = arrived[:, i].astype(F32).reshape(keys, LANES).astype(BF)
                pair_buf[i] = block
                stat[i * hp : (i + 1) * hp] = (
                    LOGIT_WEIGHT * dot_t(w16, block) + chain_col * same[i : i + 1] + masked
                )
        logits = stat[...] + (LOGIT_WEIGHT * head_dim ** (-0.5)) * scores + coef * distance
        power = jnp.exp(logits - jnp.max(logits, axis=1, keepdims=True))
        attention = (power / jnp.sum(power, axis=1, keepdims=True)).astype(BF)

        for i in range(rows):
            pair_acc[i * hp : (i + 1) * hp] = dot(attention[i * hp : (i + 1) * hp], pair_buf[i])
        outputs = collapse(dot(attention, v_bf), mask_q)
        glob = dot(attention, v_high) + dot(attention, v_low)
        shifted = [
            collapse(glob[:, c * LANES : (c + 1) * LANES], mask_v) - cols[9 + c] for c in range(3)
        ]
        local = [
            cols[c] * shifted[0] + cols[3 + c] * shifted[1] + cols[6 + c] * shifted[2]
            for c in range(3)
        ]
        norm = jnp.sqrt(local[0] * local[0] + local[1] * local[1] + local[2] * local[2] + 1e-08)
        pair_out = [pair_acc[pl.ds(h, rows, stride=hp), :].astype(BF) for h in range(heads)]

        if layer == 0:
            ready(OUTPUT_WEIGHT, GAIN_FIRST, GAIN_SECOND)
            ready(MLP_FIRST, MLP_SECOND, MLP_THIRD, FRAME_WEIGHT)
        ow = vm[OUTPUT_WEIGHT]
        at = heads * head_dim
        total = dot(outputs[:, 0:at].astype(BF), ow[0:at])
        for part in local + [norm]:
            total = total + dot(part[:, 0:pv].astype(BF), ow[at : at + pv])
            at = at + pv
        total = total + dot(jnp.concatenate(pair_out, axis=1), ow[at:])
        normed = layer_norm(state + total, vm[GAIN_FIRST][...][None])
        hidden = jnp.maximum(dot(normed.astype(BF), vm[MLP_FIRST][...]), 0.0).astype(BF)
        hidden = jnp.maximum(dot(hidden, vm[MLP_SECOND][...]), 0.0).astype(BF)
        state = layer_norm(normed + dot(hidden, vm[MLP_THIRD][...]), vm[GAIN_SECOND][...][None])
        state_bf = state.astype(BF)
        fu = dot_t(state_bf, vm[FRAME_WEIGHT][...])
        new = compose(cols, [fu[:, c : c + 1] for c in range(6)])
        frame = jnp.zeros((rows, LANES), F32)
        for c in range(12):
            frame = jnp.where(lane_rows == c, new[c], frame)
        if layer + 1 < LAYERS:
            gat[layer + 1, me, :, 0:channels] = state_bf
            gat[layer + 1, me, :, channels:] = pack_frame(frame)
            each_peer(lambda p: send_state(layer + 1, p).start())

    single_out[...] = state
    rotation_out[...] = frame[:, 0:9]
    tile[0:rows, :] = frame
    turned = tile[...].T
    translation_out[...] = turned[9:12, 0:rows]
    for layer in range(LAYERS):
        each_peer(lambda p: send_state(layer, p).wait_send())
    each_peer(lambda p: send_pair(p, me).wait_send())


ORDER = (
    PAIR_COLS,
    SINGLE,
    ROTATION,
    TRANSLATION,
    HEAD_WEIGHT,
    CHAIN_WEIGHT,
    QUERY_WEIGHT,
    QPOINT_WEIGHT,
    KEY_WEIGHT,
    KPOINT_WEIGHT,
    VALUE_WEIGHT,
    VPOINT_WEIGHT,
    PAIR_WEIGHT,
    FRAME_WEIGHT,
    CHAIN_INDEX,
    RESIDUE_MASK,
    OUTPUT_WEIGHT,
    GAIN_FIRST,
    MLP_FIRST,
    MLP_SECOND,
    MLP_THIRD,
    GAIN_SECOND,
)


def hand_out(*refs):
    for source, target in zip(refs[0:3], refs[3:6]):
        target[...] = source[...]


TURNED = (
    ROTATION,
    QUERY_WEIGHT,
    KEY_WEIGHT,
    VALUE_WEIGHT,
    QPOINT_WEIGHT,
    KPOINT_WEIGHT,
    VPOINT_WEIGHT,
    FRAME_WEIGHT,
)
PLACED = (
    QUERY_WEIGHT,
    KEY_WEIGHT,
    VALUE_WEIGHT,
    QPOINT_WEIGHT,
    KPOINT_WEIGHT,
    VPOINT_WEIGHT,
)


def on_device(*args):
    n = lax.axis_size("row")
    given = dict(enumerate(args))
    given = {k: v.reshape(1, -1) if v.ndim == 1 and k not in (GAIN_FIRST, GAIN_SECOND) else v for k, v in given.items()}
    names = list(ORDER)
    for name in TURNED:
        given[name] = given[name].T
    arrays = [given[name] for name in names]
    rows, channels = given[SINGLE].shape
    heads = given[HEAD_WEIGHT].shape[1]
    hp = up(heads, 16)
    keys = n * rows
    pair_c = given[PAIR_COLS].shape[2]
    qd = up(given[QUERY_WEIGHT].shape[0], LANES)
    stubs = PLACED
    scratch = [
        pltpu.VMEM((8, LANES) if name in stubs else given[name].shape, given[name].dtype)
        for name in names[1:]
    ] + [
        pltpu.VMEM((n, rows, rows, pair_c), BF),
        pltpu.VMEM((rows, keys, pair_c), BF),
        pltpu.VMEM((LAYERS, n, rows, channels + LANES), BF),
        pltpu.VMEM((2 * qd + 6 * LANES, channels), BF),
        pltpu.VMEM((qd + 3 * LANES, channels), BF),
        pltpu.VMEM((hp, pair_c), F32),
        pltpu.VMEM((LANES, LANES), F32),
        pltpu.VMEM((rows * hp, keys), F32),
        pltpu.VMEM((rows * hp, pair_c), F32),
        pltpu.SemaphoreType.DMA((len(names) + 5,)),
        pltpu.SemaphoreType.DMA((LAYERS, n)),
        pltpu.SemaphoreType.DMA((LAYERS, n)),
        pltpu.SemaphoreType.DMA((n,)),
        pltpu.SemaphoreType.DMA((n,)),
        pltpu.SemaphoreType.DMA,
    ]
    shapes = (
        jax.ShapeDtypeStruct((rows, channels), F32),
        jax.ShapeDtypeStruct(given[ROTATION].shape, F32),
        jax.ShapeDtypeStruct(given[TRANSLATION].shape, F32),
    )
    results = pl.pallas_call(
        functools.partial(kernel, n, names),
        name="ipa",
        out_shape=shapes,
        in_specs=[pl.BlockSpec(memory_space=pl.ANY)] * len(names),
        out_specs=[pl.BlockSpec(memory_space=pltpu.VMEM)] * 3,
        scratch_shapes=scratch,
        compiler_params=pltpu.CompilerParams(
            collective_id=0, has_side_effects=True, vmem_limit_bytes=60 * 1024 * 1024
        ),
    )(*arrays)
    state, rotation, translation = pl.pallas_call(
        hand_out,
        name="out",
        out_shape=shapes,
        in_specs=[pl.BlockSpec(memory_space=pltpu.VMEM)] * 3,
        out_specs=[pl.BlockSpec(memory_space=pltpu.VMEM)] * 3,
    )(*results)
    return state, rotation.T, translation


def solution(mesh):
    split = P(None, ("groups", "row"))
    return jax.shard_map(
        on_device,
        mesh=mesh,
        in_specs=(
            P(None, ("groups", "row"), None),
            P(("groups", "row"), None),
            split,
            split,
            P("groups"),
            P("groups"),
        )
        + (P(),) * 16,
        out_specs=(P(("groups", "row"), None), split, split),
        check_vma=False,
    )
```

time: 73.8 us -> 30.3 us (0.41)
  blocking collectives: 40.7 us -> 0 us
  Pallas kernels: 0 us -> 29.5 us
  matrix products: 11.1 us -> 0 us
  local copies, waits for them, and re-layouts: 8.4 us -> 0 us
  starting transfers between devices: 7.53 us -> 0 us
  other arithmetic: 4.2 us -> 0 us
    all_gather x2 -> x0, blocking collectives: 40.7 us -> none  [on_device(): gathered = lax.all_gather(packed, 'row', axis=0, tiled=True)]
    pallas_call x0 -> x2, Pallas kernels: none -> 29.5 us  [the longest x1 28.1 us: on_device(): pl.pallas_call(functools.partial(kernel, n, names), name='ipa', out_shape...]
    dot_general x29 -> x0, matrix products: 10.5 us -> none  [the longest x2 2.49 us: update(): jnp.dot(hidden, mlp_third, preferred_element_type=jnp.float32)]
    all_to_all x1 -> x0, starting transfers between devices: 7.53 us -> none  [on_device(): lax.all_to_all(blocks, 'row', split_axis=0, concat_axis=2, tiled=True)[0]]
    slice x6 -> x0, local copies, waits for them, and re-layouts: 2.53 us -> none  [the longest x3 2.07 us: to_global(): translation[component][:, None]]
    unnamed x44 -> x0, local copies, waits for them, and re-layouts: 1.62 us -> none
    convert_element_type x5 -> x0, other arithmetic: 1.01 us -> none  [the longest x1 0.69 us: on_device(): single_state = single.astype(jnp.float32)]
    squeeze x13 -> x0, local copies, waits for them, and re-layouts: 0.98 us -> none  [the longest x3 0.17 us: frame_compose(): frame_update[:, 3]]
  transfers between devices with their start and end apart: 1 -> 0, of which waited for: 0 -> 0; matrix products, arithmetic and copies ran while one was open for 10% -> 0% of each run, Pallas kernels for 0% -> 0%
where the time goes in v1:
time: 30.3 us; the launch traced here: 30.1 us
  Pallas kernels  29.5 us (97%)
  between operations  0.65 us (2%)
    pallas_call x1, Pallas kernels, on_device(): pl.pallas_call(functools.partial(kernel, n, names), name='ipa', out_shape...  28.1 us
    pallas_call x1, Pallas kernels, on_device(): pl.pallas_call(hand_out, name='out', out_shape=shapes, in_specs=[pl.Block...  1.32 us

profile of v1, /device:TPU:0, one launch (start us, length us, event | category | flops | bytes accessed | tf_op | source)
XLA Modules:
  0.0 30.1 jit_solution(15229701298491580820)
XLA Ops:
  0.6 28.1 %ipa.1 = (f32[8,384]{1,0:T(8,128)}, f32[8,9]{1,0:T(8,128)}, f32[3,8]{1,0:T(4,128)}) custom-call(bf16[128,8,128]{2,1,0:T(8,128)(2,1)} %refs_0_.1, bf16[8,384]{1,0:T(8,128)(2,1)} %refs_1_.1, f32[8,9]{1,0:T(8,128)} %bitcast.20, f32[3,8]{1,0:T(4,128)} %refs_3_.1, f32[1,12]{1,0:T(1,128)} %bitcast.21, f32[1,12]{1,0:T(1,128)} %bitcast.22, ...), custom_call_target="tpu_custom_call" | custom-call | tf_op jit(solution)/shard_map/ipa/pallas_call | solution.py:483
  28.8 1.3 %out.1 = (f32[8,384]{1,0:T(8,128)}, f32[8,9]{1,0:T(8,128)}, f32[3,8]{1,0:T(4,128)}) custom-call(f32[8,384]{1,0:T(8,128)} %get-tuple-element.9.refs_0_, f32[8,9]{1,0:T(8,128)} %get-tuple-element.10.refs_1_, f32[3,8]{1,0:T(4,128)} %get-tuple-element.11.refs_2_), custom_call_target="tpu_custom_call" | custom-call | tf_op jit(solution)/shard_map/out/pallas_call | solution.py:494
